TPU v7x, 512 devices: a whole 4x8x8 slice. The times are simulated.
512 devices in a mesh: bin: 64 (over z, x, y_hi), grp: 8 (over y_lo, core).
Axes of the slice: x: 4, y: 8 (y_hi: 2, y_lo: 4; y = y_hi * 4 + y_lo), z: 8, core: 2. Of those that a mesh axis runs over, the one named last changes fastest.
Arguments:
- record: bfloat16 [8, 256, 8704], P('grp', 'bin'), may hold values from -60 to 60
- ref_index: int32 [8, 16], P('grp'), may hold values from 0 to 255, as said below
- offsets: int32 [16], replicated, may hold values from 0 to 7680, as said below
Outputs:
- transfer: bfloat16 [512, 2048, 256], P('bin', 'grp')
Inputs may be any that keep to these rules, and one draw needn't show every extreme that they name: `ref_index`: each row lists 16 different channels of its group; every row holds 0 and 255. `offsets`: starts rise; the first is 0, the last is 7680, and neighbours lie 512 // 2 to 768 apart.
All inputs are finite; a program needn't handle non-finite values.
Results may differ from a plain program's by a relative error of at most 0.0095.
Values may be sent and summed in bfloat16 or wider, within the bound.
A program may use at most 64 MiB of HBM per device.

v0:
```python
import math
import jax
import jax.numpy as jnp
from jax import lax
from jax.sharding import PartitionSpec as P

L = 1024
NB = 512
ridge_weight = 0.5


def make_table(seg_len, bins):
    sample_num = lax.iota(jnp.int32, seg_len)[:, None]
    bin_num = lax.iota(jnp.int32, bins)[None, :]
    angles = (sample_num * bin_num % seg_len).astype(jnp.float32) * (2.0 * math.pi / seg_len)
    hann_window = 0.5 - 0.5 * jnp.cos(sample_num.astype(jnp.float32) * (2.0 * math.pi / seg_len))
    return jnp.concatenate(
        [hann_window * jnp.cos(angles), -(hann_window * jnp.sin(angles))], axis=1
    ).astype(jnp.bfloat16)


def transform(chan_rows, starts, dft_table, bin_devices):
    seg_len = dft_table.shape[0]
    pieces = jax.vmap(lambda start_at: lax.dynamic_slice_in_dim(chan_rows, start_at, seg_len, 1))(
        starts
    )
    spectra = jnp.einsum(
        "scn,nk->ksc", pieces, dft_table, preferred_element_type=jnp.float32
    ).astype(jnp.bfloat16)
    bin_total = dft_table.shape[1] // 2
    return spectra.reshape(
        2, bin_devices, bin_total // bin_devices, starts.shape[0], chan_rows.shape[0]
    )


def local(record, ref_index, offsets):
    chan_rows = record[0]
    dft_table = make_table(L, NB)
    bin_devices = lax.axis_size("bin")
    spectra = transform(chan_rows, offsets, dft_table, bin_devices)
    channels = lax.all_to_all(spectra, "bin", split_axis=1, concat_axis=4, tiled=True)[:, 0]
    local_refs = jnp.take(channels, ref_index[0], axis=3)
    references = lax.all_gather(local_refs, "grp", axis=3, tiled=True)
    ref_real = references[0]
    ref_imag = references[1]
    ref_blocks = jnp.stack(
        [
            jnp.concatenate([ref_real, -ref_imag], axis=-1),
            jnp.concatenate([ref_imag, ref_real], axis=-1),
        ]
    )
    bins_here = channels.shape[1]
    group_size = math.gcd(bins_here, 4)
    group_count = bins_here // group_size
    real_order = ref_blocks.shape[-1]

    def solve_group(group_index):
        first_bin = group_index * group_size
        ref_group = lax.dynamic_slice_in_dim(ref_blocks, first_bin, group_size, 1)
        chan_group = lax.dynamic_slice_in_dim(channels, first_bin, group_size, 1)
        cross_part = jnp.einsum(
            "pfsr,pfsc->frc", ref_group, chan_group, preferred_element_type=jnp.float32
        )
        auto_part = jnp.einsum(
            "pfsr,pfsq->frq", ref_group, ref_group, preferred_element_type=jnp.float32
        )
        ridge_term = ridge_weight * jnp.trace(auto_part, axis1=1, axis2=2) / real_order
        factor = jnp.linalg.cholesky(
            auto_part + ridge_term[:, None, None] * jnp.eye(real_order, dtype=jnp.float32)
        )
        transfer_t = jax.scipy.linalg.cho_solve((factor, True), cross_part)
        return jnp.swapaxes(transfer_t, 1, 2).astype(jnp.bfloat16)

    results = lax.map(solve_group, jnp.arange(group_count))
    return results.reshape(bins_here, results.shape[2], results.shape[3])


def solution(mesh):
    placed = (P("grp", "bin", None), P("grp", None), P())
    return jax.shard_map(
        local, mesh=mesh, in_specs=placed, out_specs=P("bin", "grp", None), check_vma=False
    )
```

profile of v0, /device:TPU:1, one launch (start us, length us, event | category | flops | bytes accessed | tf_op | source)
XLA Modules:
  0.0 550.2 jit_solution(7552281096765540275)
XLA Ops:
  0.1 8.9 %multiply_convert_fusion = (bf16[1024,512]{1,0:T(8,128)(2,1)S(1)}, bf16[1024,512]{1,0:T(8,128)(2,1)S(1)}) fusion(f32[1024]{0:T(1024)S(1)} %multiply_subtract_fusion), kind=kLoop, calls=%fused_computation.58 | loop fusion | flops 9961472 | bytes 2101248 | tf_op jit(solution)/shard_map/convert.2
  9.0 32.3 %while.17 = (s32[]{:T(128)}, bf16[4,8704]{1,0:T(4,128)(2,1)}, s32[16,2]{0,1:T(2,128)S(1)}, bf16[16,4,1024]{2,1,0:T(4,128)(2,1)S(1)}, s32[]{:T(128)}) while((s32[]{:T(128)}, bf16[4,8704]{1,0:T(4,128)(2,1)}, s32[16,2]{0,1:T(2,128)S(1)}, bf16[16,4,1024]{2,1,0:T(4,128)(2,1)S(1)}, s32[]{:T(128)}) %tuple.87), condition=%wide.while_cond.1, body=%wide.while_body.1.sunk | while | flops 2 | bytes 16481 | solution.py:24
  9.6 1.4 bitcast_dynamic-update-slice_fusion.4
  11.6 1.4 bitcast_dynamic-update-slice_fusion.4
  13.6 1.4 bitcast_dynamic-update-slice_fusion.4
  15.7 1.4 bitcast_dynamic-update-slice_fusion.4
  17.7 1.4 bitcast_dynamic-update-slice_fusion.4
  19.7 1.4 bitcast_dynamic-update-slice_fusion.4
  21.7 1.4 bitcast_dynamic-update-slice_fusion.4
  23.7 1.4 bitcast_dynamic-update-slice_fusion.4
  25.7 1.4 bitcast_dynamic-update-slice_fusion.4
  27.7 1.4 bitcast_dynamic-update-slice_fusion.4
  29.8 1.4 bitcast_dynamic-update-slice_fusion.4
  31.8 1.4 bitcast_dynamic-update-slice_fusion.4
  33.8 1.4 bitcast_dynamic-update-slice_fusion.4
  35.8 1.4 bitcast_dynamic-update-slice_fusion.4
  39.8 1.4 bitcast_dynamic-update-slice_fusion.4
  42.5 1.8 reshape.166
  44.3 19.6 %all-to-all-start = ((bf16[64,2,512]{2,1,0:T(2,128)(2,1)}), bf16[64,2,512]{2,1,0:T(2,128)(2,1)S(1)}, u32[]{:S(2)}, u32[]{:S(2)}) async-start(bf16[64,2,512]{2,1,0:T(2,128)(2,1)} %reshape.166), calls=%async_computation | async-start | bytes 262144 | tf_op jit(solution)/shard_map/all_to_all | solution.py:41
  63.9 13.6 %all-to-all-done = bf16[64,2,512]{2,1,0:T(2,128)(2,1)S(1)} async-done(((bf16[64,2,512]{2,1,0:T(2,128)(2,1)}), bf16[64,2,512]{2,1,0:T(2,128)(2,1)S(1)}, u32[]{:S(2)}, u32[]{:S(2)}) %all-to-all-start) | async-done | bytes 131104 | tf_op jit(solution)/shard_map/all_to_all | solution.py:41
  79.2 16.7 %all_gather.3 = bf16[2,8,16,128]{2,1,0,3:T(8,128)(2,1)S(1)} all-gather(bf16[2,8,16,16]{2,1,0,3:T(8,128)(2,1)S(1)} %select_bitcast_fusion.1), channel_id=1, replica_groups=mesh['bin'=64,'grp'=8] {'grp'}, dimensions={3}, use_global_device_ids=true | all-gather | bytes 73728 | tf_op jit(solution)/shard_map/all_gather | solution.py:43
  97.5 452.7 %while.16 = (s32[]{:T(128)}, bf16[2,4,256,256]{3,2,1,0:T(8,128)(2,1)}, s32[2]{0:T(128)S(1)}, bf16[2,8,16,256]{3,2,1,0:T(8,128)(2,1)S(1)}, bf16[2,8,16,256]{3,2,0...) while((s32[]{:T(128)}, ...), condition=%wide.region_6.7_spmd, body=%wide.region_0.6_spmd.sunk | while | flops 1448117248 | bytes 37234176 | solution.py:74
  100.1 46.9 %custom-call.42 = f32[4,128,128]{2,1,0:T(8,128)S(1)} custom-call(f32[4,128,128]{2,1,0:T(8,128)S(1)} %cholesky.172), custom_call_target="Cholesky" | custom-call | tf_op jit(solution)/shard_map/while/body/eval_jaxpr/jit(cholesky)/cholesky | solution.py:68
  147.1 39.3 %custom-call.43 = f32[4,1,128,128]{2,3,1,0:T(8,128)S(1)} custom-call(f32[4,1,128,128]{3,2,1,0:T(8,128)S(1)} %select_bitcast_fusion.3), custom_call_target="InvertDiagBlocksLowerTriangular" | custom-call | tf_op jit(solution)/shard_map/while/body/eval_jaxpr/jit(cholesky)/cholesky | solution.py:68
  187.5 46.9 %custom-call.44 = f32[4,128,128]{2,1,0:T(8,128)S(1)} custom-call(f32[4,128,128]{2,1,0:T(8,128)S(1)} %convolution_subtract_fusion.6), custom_call_target="Cholesky" | custom-call | tf_op jit(solution)/shard_map/while/body/eval_jaxpr/jit(cholesky)/cholesky | solution.py:68
  235.1 3.9 while.18
  239.0 78.6 %custom-call.46 = f32[4,2,128,128]{2,3,1,0:T(8,128)S(1)} custom-call(f32[4,2,128,128]{3,2,1,0:T(8,128)S(1)} %bitcast.144), custom_call_target="InvertDiagBlocksLowerTriangular" | custom-call | tf_op jit(solution)/shard_map/while/body/eval_jaxpr/jit(_cho_solve)/vmap()/triangular_solve | solution.py:71
  326.3 46.9 %custom-call.42 = f32[4,128,128]{2,1,0:T(8,128)S(1)} custom-call(f32[4,128,128]{2,1,0:T(8,128)S(1)} %cholesky.172), custom_call_target="Cholesky" | custom-call | tf_op jit(solution)/shard_map/while/body/eval_jaxpr/jit(cholesky)/cholesky | solution.py:68
  373.4 39.3 %custom-call.43 = f32[4,1,128,128]{2,3,1,0:T(8,128)S(1)} custom-call(f32[4,1,128,128]{3,2,1,0:T(8,128)S(1)} %select_bitcast_fusion.3), custom_call_target="InvertDiagBlocksLowerTriangular" | custom-call | tf_op jit(solution)/shard_map/while/body/eval_jaxpr/jit(cholesky)/cholesky | solution.py:68
  413.8 46.9 %custom-call.44 = f32[4,128,128]{2,1,0:T(8,128)S(1)} custom-call(f32[4,128,128]{2,1,0:T(8,128)S(1)} %convolution_subtract_fusion.6), custom_call_target="Cholesky" | custom-call | tf_op jit(solution)/shard_map/while/body/eval_jaxpr/jit(cholesky)/cholesky | solution.py:68
  461.3 3.9 while.18
  465.3 78.6 %custom-call.46 = f32[4,2,128,128]{2,3,1,0:T(8,128)S(1)} custom-call(f32[4,2,128,128]{3,2,1,0:T(8,128)S(1)} %bitcast.144), custom_call_target="InvertDiagBlocksLowerTriangular" | custom-call | tf_op jit(solution)/shard_map/while/body/eval_jaxpr/jit(_cho_solve)/vmap()/triangular_solve | solution.py:71
  (148 shorter events, 43.1 us)
Async XLA Ops:
  0.1 8.9 %copy-start.2 = (s32[16]{0:T(128)S(1)}, s32[16]{0:T(128)}, u32[]{:S(2)}) copy-start(s32[16]{0:T(128)} %param.7) | copy-start | bytes 196
  42.5 21.4 %copy-start.3 = (s32[1,16]{1,0:T(1,128)S(1)}, s32[1,16]{1,0:T(1,128)}, u32[]{:S(2)}) copy-start(s32[1,16]{1,0:T(1,128)} %param.6) | copy-start | bytes 196
  44.3 33.2 %all-to-all-start = ((bf16[64,2,512]{2,1,0:T(2,128)(2,1)}), bf16[64,2,512]{2,1,0:T(2,128)(2,1)S(1)}, u32[]{:S(2)}, u32[]{:S(2)}) async-start(bf16[64,2,512]{2,1,0:T(2,128)(2,1)} %reshape.166), calls=%async_computation | async-start | bytes 262144 | tf_op jit(solution)/shard_map/all_to_all | solution.py:41
  321.7 1.2 copy-start
  322.9 1.0 copy-start.1
  547.9 1.2 copy-start
  549.2 1.0 copy-start.1
where the time goes:
time: 552 us; the launch traced here: 550 us
  other arithmetic  435 us (79%)
  local copies, waits for them, and re-layouts  52.2 us (9%)
  starting transfers between devices  19.6 us (4%)
  blocking collectives  16.7 us (3%)
  waiting for transfers between devices  13.6 us (2%)
  matrix products  11.5 us (2%)
    another operation x20, other arithmetic, solve_group(): jnp.linalg.cholesky(auto_part + ridge_term[:, None, None] * jnp.eye(real_...  267 us
    another operation x8, other arithmetic, solve_group(): transfer_t = jax.scipy.linalg.cho_solve((factor, True), cross_part)  158 us
    gather x48, local copies, waits for them, and re-layouts  32.2 us
    all_to_all x1, starting transfers between devices, local(): lax.all_to_all(spectra, 'bin', split_axis=1, concat_axis=4, tiled=True)  19.6 us
    all_gather x1, blocking collectives, local(): references = lax.all_gather(local_refs, 'grp', axis=3, tiled=True)  16.7 us
    all_to_all x1, waiting for transfers between devices, local(): lax.all_to_all(spectra, 'bin', split_axis=1, concat_axis=4, tiled=True)  13.6 us
  transfers between devices with their start and end apart: 1, of which 1 were waited for; matrix products, arithmetic and copies ran while one was open for 0% of the time, Pallas kernels for 0%

commit v1 on v0

--- a/solution.py
+++ b/solution.py
@@ -40,7 +40,9 @@
     spectra = transform(chan_rows, offsets, dft_table, bin_devices)
     channels = lax.all_to_all(spectra, "bin", split_axis=1, concat_axis=4, tiled=True)[:, 0]
     local_refs = jnp.take(channels, ref_index[0], axis=3)
-    references = lax.all_gather(local_refs, "grp", axis=3, tiled=True)
+    references = jnp.concatenate(
+        lax.all_to_all(jnp.stack([local_refs] * lax.axis_size("grp")), "grp", 0, 0), axis=3
+    )
     ref_real = references[0]
     ref_imag = references[1]
     ref_blocks = jnp.stack(

time: 552 us -> 544 us (0.986)
  blocking collectives: 16.7 us -> 0 us
    all_gather x1 -> x0, blocking collectives: 16.7 us -> none  [local(): references = lax.all_gather(local_refs, 'grp', axis=3, tiled=True)]
  transfers between devices with their start and end apart: 1 -> 2, of which waited for: 1 -> 2; matrix products, arithmetic and copies ran while one was open for 0% -> 0% of each run, Pallas kernels for 0% -> 0%
where the time goes in v1:
time: 544 us; the launch traced here: 543 us
  other arithmetic  434 us (80%)
  local copies, waits for them, and re-layouts  52.4 us (10%)
  starting transfers between devices  24.8 us (5%)
  waiting for transfers between devices  17.8 us (3%)
  matrix products  11.4 us (2%)
    another operation x20, other arithmetic, solve_group(): jnp.linalg.cholesky(auto_part + ridge_term[:, None, None] * jnp.eye(real_...  267 us
    another operation x8, other arithmetic, solve_group(): transfer_t = jax.scipy.linalg.cho_solve((factor, True), cross_part)  158 us
    gather x48, local copies, waits for them, and re-layouts  30.8 us
    all_to_all x1, starting transfers between devices, local(): lax.all_to_all(spectra, 'bin', split_axis=1, concat_axis=4, tiled=True)  19.6 us
    all_to_all x1, waiting for transfers between devices, local(): lax.all_to_all(spectra, 'bin', split_axis=1, concat_axis=4, tiled=True)  13.6 us
  transfers between devices with their start and end apart: 2, of which 2 were waited for; matrix products, arithmetic and copies ran while one was open for 0% of the time, Pallas kernels for 0%

profile of v1, /device:TPU:1, one launch (start us, length us, event | category | flops | bytes accessed | tf_op | source)
XLA Modules:
  0.0 543.1 jit_solution(13197831088162692127)
XLA Ops:
  0.1 8.9 %multiply_convert_fusion = (bf16[1024,512]{1,0:T(8,128)(2,1)S(1)}, bf16[1024,512]{1,0:T(8,128)(2,1)S(1)}) fusion(f32[1024]{0:T(1024)S(1)} %multiply_subtract_fusion), kind=kLoop, calls=%fused_computation.58 | loop fusion | flops 9961472 | bytes 2101248 | tf_op jit(solution)/shard_map/convert.2
  9.0 30.9 %while.17 = (s32[]{:T(128)}, bf16[4,8704]{1,0:T(4,128)(2,1)}, s32[16,2]{0,1:T(2,128)S(1)}, bf16[16,4,1024]{2,1,0:T(4,128)(2,1)S(1)}, s32[]{:T(128)}) while((s32[]{:T(128)}, bf16[4,8704]{1,0:T(4,128)(2,1)}, s32[16,2]{0,1:T(2,128)S(1)}, bf16[16,4,1024]{2,1,0:T(4,128)(2,1)S(1)}, s32[]{:T(128)}) %tuple.87), condition=%wide.while_cond.1, body=%wide.while_body.1.sunk | while | flops 2 | bytes 16481 | solution.py:24
  9.6 1.3 bitcast_dynamic-update-slice_fusion.4
  11.5 1.3 bitcast_dynamic-update-slice_fusion.4
  13.4 1.3 bitcast_dynamic-update-slice_fusion.4
  15.4 1.3 bitcast_dynamic-update-slice_fusion.4
  17.3 1.3 bitcast_dynamic-update-slice_fusion.4
  19.2 1.3 bitcast_dynamic-update-slice_fusion.4
  21.1 1.3 bitcast_dynamic-update-slice_fusion.4
  23.1 1.3 bitcast_dynamic-update-slice_fusion.4
  25.0 1.3 bitcast_dynamic-update-slice_fusion.4
  26.9 1.3 bitcast_dynamic-update-slice_fusion.4
  28.9 1.3 bitcast_dynamic-update-slice_fusion.4
  30.8 1.3 bitcast_dynamic-update-slice_fusion.4
  32.7 1.3 bitcast_dynamic-update-slice_fusion.4
  38.5 1.4 bitcast_dynamic-update-slice_fusion.4
  41.1 1.8 reshape.177
  42.9 19.6 %all-to-all-start = ((bf16[64,2,512]{2,1,0:T(2,128)(2,1)}), bf16[64,2,512]{2,1,0:T(2,128)(2,1)S(1)}, u32[]{:S(2)}, u32[]{:S(2)}) async-start(bf16[64,2,512]{2,1,0:T(2,128)(2,1)} %reshape.177), calls=%async_computation | async-start | bytes 262144 | tf_op jit(solution)/shard_map/all_to_all | solution.py:41
  62.6 13.6 %all-to-all-done = bf16[64,2,512]{2,1,0:T(2,128)(2,1)S(1)} async-done(((bf16[64,2,512]{2,1,0:T(2,128)(2,1)}), bf16[64,2,512]{2,1,0:T(2,128)(2,1)S(1)}, u32[]{:S(2)}, u32[]{:S(2)}) %all-to-all-start) | async-done | bytes 131104 | tf_op jit(solution)/shard_map/all_to_all | solution.py:41
  79.3 5.2 all-to-all-start.1
  85.4 4.3 all-to-all-done.1
  90.9 452.2 %while.16 = (s32[]{:T(128)}, bf16[2,4,256,256]{3,2,1,0:T(8,128)(2,1)}, s32[2]{0:T(128)S(1)}, bf16[2,8,16,256]{3,2,1,0:T(8,128)(2,1)S(1)}, bf16[2,8,16,256]{3,2,0...) while((s32[]{:T(128)}, ...), condition=%wide.region_6.7_spmd, body=%wide.region_0.6_spmd.sunk | while | flops 1448117248 | bytes 37234176 | solution.py:76
  93.4 46.9 %custom-call.42 = f32[4,128,128]{2,1,0:T(8,128)S(1)} custom-call(f32[4,128,128]{2,1,0:T(8,128)S(1)} %cholesky.172), custom_call_target="Cholesky" | custom-call | tf_op jit(solution)/shard_map/while/body/eval_jaxpr/jit(cholesky)/cholesky | solution.py:70
  140.5 39.3 %custom-call.43 = f32[4,1,128,128]{2,3,1,0:T(8,128)S(1)} custom-call(f32[4,1,128,128]{3,2,1,0:T(8,128)S(1)} %select_bitcast_fusion.3), custom_call_target="InvertDiagBlocksLowerTriangular" | custom-call | tf_op jit(solution)/shard_map/while/body/eval_jaxpr/jit(cholesky)/cholesky | solution.py:70
  180.9 46.9 %custom-call.44 = f32[4,128,128]{2,1,0:T(8,128)S(1)} custom-call(f32[4,128,128]{2,1,0:T(8,128)S(1)} %convolution_subtract_fusion.6), custom_call_target="Cholesky" | custom-call | tf_op jit(solution)/shard_map/while/body/eval_jaxpr/jit(cholesky)/cholesky | solution.py:70
  228.4 3.7 while.18
  232.2 78.6 %custom-call.46 = f32[4,2,128,128]{2,3,1,0:T(8,128)S(1)} custom-call(f32[4,2,128,128]{3,2,1,0:T(8,128)S(1)} %bitcast.144), custom_call_target="InvertDiagBlocksLowerTriangular" | custom-call | tf_op jit(solution)/shard_map/while/body/eval_jaxpr/jit(_cho_solve)/vmap()/triangular_solve | solution.py:73
  319.4 46.9 %custom-call.42 = f32[4,128,128]{2,1,0:T(8,128)S(1)} custom-call(f32[4,128,128]{2,1,0:T(8,128)S(1)} %cholesky.172), custom_call_target="Cholesky" | custom-call | tf_op jit(solution)/shard_map/while/body/eval_jaxpr/jit(cholesky)/cholesky | solution.py:70
  366.5 39.3 %custom-call.43 = f32[4,1,128,128]{2,3,1,0:T(8,128)S(1)} custom-call(f32[4,1,128,128]{3,2,1,0:T(8,128)S(1)} %select_bitcast_fusion.3), custom_call_target="InvertDiagBlocksLowerTriangular" | custom-call | tf_op jit(solution)/shard_map/while/body/eval_jaxpr/jit(cholesky)/cholesky | solution.py:70
  406.9 46.9 %custom-call.44 = f32[4,128,128]{2,1,0:T(8,128)S(1)} custom-call(f32[4,128,128]{2,1,0:T(8,128)S(1)} %convolution_subtract_fusion.6), custom_call_target="Cholesky" | custom-call | tf_op jit(solution)/shard_map/while/body/eval_jaxpr/jit(cholesky)/cholesky | solution.py:70
  454.4 3.7 while.18
  458.2 78.6 %custom-call.46 = f32[4,2,128,128]{2,3,1,0:T(8,128)S(1)} custom-call(f32[4,2,128,128]{3,2,1,0:T(8,128)S(1)} %bitcast.144), custom_call_target="InvertDiagBlocksLowerTriangular" | custom-call | tf_op jit(solution)/shard_map/while/body/eval_jaxpr/jit(_cho_solve)/vmap()/triangular_solve | solution.py:73
  (154 shorter events, 45.3 us)
Async XLA Ops:
  0.1 8.9 %copy-start.2 = (s32[16]{0:T(128)S(1)}, s32[16]{0:T(128)}, u32[]{:S(2)}) copy-start(s32[16]{0:T(128)} %param.7) | copy-start | bytes 196
  41.1 21.4 %copy-start.3 = (s32[1,16]{1,0:T(1,128)S(1)}, s32[1,16]{1,0:T(1,128)}, u32[]{:S(2)}) copy-start(s32[1,16]{1,0:T(1,128)} %param.6) | copy-start | bytes 196
  42.9 33.2 %all-to-all-start = ((bf16[64,2,512]{2,1,0:T(2,128)(2,1)}), bf16[64,2,512]{2,1,0:T(2,128)(2,1)S(1)}, u32[]{:S(2)}, u32[]{:S(2)}) async-start(bf16[64,2,512]{2,1,0:T(2,128)(2,1)} %reshape.177), calls=%async_computation | async-start | bytes 262144 | tf_op jit(solution)/shard_map/all_to_all | solution.py:41
  79.3 10.4 %all-to-all-start.1 = ((bf16[8,2,2048]{2,1,0:T(2,128)(2,1)}), bf16[8,2,2048]{2,1,0:T(2,128)(2,1)S(1)}, u32[]{:S(2)}, u32[]{:S(2)}) async-start(bf16[8,2,2048]{2,1,0:T(2,128)(2,1)} %reshape.179), calls=%async_computation.1 | async-start | bytes 131072 | tf_op jit(solution)/shard_map/all_to_all | solution.py:44
  314.9 1.2 copy-start
  316.1 1.0 copy-start.1
  540.8 1.2 copy-start
  542.1 1.0 copy-start.1
